TPU v7x, 128 devices: a whole 4x4x4 slice. The times are simulated.
128 devices in a mesh: pix: 8 (over y_hi, x), mode: 16 (over z, y_lo, core).
Axes of the slice: x: 4, y: 4 (y_hi: 2, y_lo: 2; y = y_hi * 2 + y_lo), z: 4, core: 2. Of those that a mesh axis runs over, the one named last changes fastest.
Arguments:
- matrix: float32 [2, 4096, 32768], P(None, 'pix', 'mode'), may hold values from -0.03125 to 0.03125
- calibration_fields: float32 [2, 4096, 512], P(None, 'pix', 'mode'), may hold values from -0.25 to 0.25
- patterns: int32 [32768, 512], P('mode'), may hold values from 0 to 255
- targets: int32 [4096, 128], P('pix'), may hold values from 0 to 255
- phases: float32 [32768, 128], P('mode'), may hold values from -3.140625 to 3.140625
Outputs:
- updated: float32 [2, 4096, 32768], P(None, 'pix', 'mode')
- slm_field: float32 [2, 32768, 128], P(None, 'mode')
- camera_field: float32 [2, 4096, 128], P(None, 'pix')
All inputs are finite; a program needn't handle non-finite values.
Results may differ from a plain program's by a relative error of at most 0.00014.
Values sent between devices are 32-bit elements; how exact they have to be, the bound alone decides.
No kernel may reach another device: no remote copies, remote signals or barrier semaphores. Data moves between devices by JAX's collectives and lax.ppermute only.
A program may use at most 128 MiB of HBM per device.

v0:
```python
import math
import jax
import jax.numpy as jnp
from jax import lax
from jax.sharding import PartitionSpec as P

LEVELS = 256
ITERS = 2


def matmul(left, right):
    return jnp.dot(left, right, precision=lax.Precision.HIGHEST, preferred_element_type=jnp.float32)


def matmul_nt(left, right):
    return lax.dot_general(
        left,
        right,
        (((1,), (1,)), ((), ())),
        precision=lax.Precision.HIGHEST,
        preferred_element_type=jnp.float32,
    )


def matmul_tn(left, right):
    return lax.dot_general(
        left,
        right,
        (((0,), (0,)), ((), ())),
        precision=lax.Precision.HIGHEST,
        preferred_element_type=jnp.float32,
    )


def camera_rows(real_new, imag_new, slm_now, width):
    real_times = matmul(real_new, slm_now)
    imag_times = matmul(imag_new, slm_now)
    return jnp.concatenate(
        [
            real_times[:, :width] - imag_times[:, width:],
            real_times[:, width:] + imag_times[:, :width],
        ],
        axis=1,
    )


def slm_rows(real_new, imag_new, shaped, width):
    real_times = matmul_tn(real_new, shaped)
    imag_times = matmul_tn(imag_new, shaped)
    return jnp.concatenate(
        [
            real_times[:, :width] + imag_times[:, width:],
            real_times[:, width:] - imag_times[:, :width],
        ],
        axis=1,
    )


def clamp_scale(source, floor_value, width):
    magnitude = jnp.sqrt(
        source[:, :width] * source[:, :width] + source[:, width:] * source[:, width:]
    )
    return 1.0 / jnp.maximum(magnitude, floor_value)


def project(camera, amplitude, width):
    factor = amplitude * clamp_scale(camera, 0.5, width)
    return camera * jnp.concatenate([factor, factor], axis=1)


def normalize(back_field, floor_value, width):
    factor = clamp_scale(back_field, floor_value, width)
    return back_field * jnp.concatenate([factor, factor], axis=1)


def camera_pass(real_new, imag_new, slm_now, amplitude, width, shaping):
    camera = lax.psum(camera_rows(real_new, imag_new, slm_now, width), "mode")
    if shaping:
        camera = project(camera, amplitude, width)
    return camera


def slm_pass(real_new, imag_new, shaped, floor_value, width):
    back_field = lax.psum(slm_rows(real_new, imag_new, shaped, width), "pix")
    slm_now = normalize(back_field, floor_value, width)
    return slm_now


def body(matrix, calibration_fields, patterns, targets, phases):
    real_start = matrix[0]
    imag_start = matrix[1]
    pix_rows, mode_cols = real_start.shape
    pix_total = pix_rows * lax.axis_size("pix")
    mode_total = mode_cols * lax.axis_size("mode")
    width = targets.shape[1]
    angles = patterns.astype(jnp.float32) * (2.0 * math.pi / LEVELS)
    cosine = jnp.cos(angles) / math.sqrt(mode_total)
    sine_table = jnp.sin(angles) / math.sqrt(mode_total)
    panel_whole = lax.all_gather(calibration_fields, "mode", axis=2, tiled=True)
    real_new = real_start + (
        matmul_nt(panel_whole[0], cosine) + matmul_nt(panel_whole[1], sine_table)
    )
    imag_new = imag_start + (
        matmul_nt(panel_whole[1], cosine) - matmul_nt(panel_whole[0], sine_table)
    )
    amplitude = targets.astype(jnp.float32) / 128.0
    floor_value = 0.5 * math.sqrt(pix_total / mode_total)
    slm_now = jnp.concatenate([jnp.cos(phases), jnp.sin(phases)], axis=1)
    for repeat in range(ITERS):
        shaped = camera_pass(real_new, imag_new, slm_now, amplitude, width, True)
        slm_now = slm_pass(real_new, imag_new, shaped, floor_value, width)
    camera = camera_pass(real_new, imag_new, slm_now, amplitude, width, False)
    updated = jnp.stack([real_new, imag_new])
    slm_field = jnp.stack([slm_now[:, :width], slm_now[:, width:]])
    camera_field = jnp.stack([camera[:, :width], camera[:, width:]])
    return (updated, slm_field, camera_field)


def solution(mesh):
    in_specs = (
        P(None, "pix", "mode"),
        P(None, "pix", "mode"),
        P("mode", None),
        P("pix", None),
        P("mode", None),
    )
    out_specs = (P(None, "pix", "mode"), P(None, "mode", None), P(None, "pix", None))
    return jax.shard_map(body, mesh=mesh, in_specs=in_specs, out_specs=out_specs, check_vma=False)
```

profile of v0, /device:TPU:1, one launch (start us, length us, event | category | flops | bytes accessed | tf_op | source)
XLA Modules:
  0.0 747.0 jit_solution(13222708839434813150)
XLA Ops:
  7.9 7.9 %fusion.54 = (f32[1,512,2048]{2,1,0:T(8,128)}, f32[1,512,2048]{2,1,0:T(8,128)}) fusion(f32[2,512,2048]{2,1,0:T(8,128)} %param.5), kind=kLoop, calls=%fused_computation.97 | loop fusion | bytes 16777216 | tf_op jit(solution)/shard_map/slice | solution.py:90
  15.8 5.5 copy.14
  21.3 5.5 copy.15
  30.5 16.7 %all-gather.2.cloned.1.call-done = f32[2,512,512]{1,2,0:T(8,128)} async-done(((f32[2,512,32]{1,2,0:T(8,128)}), f32[2,512,512]{1,2,0:T(8,128)}) %all-gather.2.cloned.1.call-update) | async-done | bytes 2097168 | tf_op jit(solution)/shard_map/all_gather | solution.py:99
  47.2 22.6 %fusion.1 = f32[2048,512]{1,0:T(8,128)S(1)} fusion(s32[2048,512]{1,0:T(8,128)} %param.7, f32[2,512,512]{1,2,0:T(8,128)} %all-gather.2.cloned.1.call-done), kind=kOutput, calls=%fused_computation.7 | convolution fusion | flops 6445596672 | bytes 9437184 | tf_op jit(solution)/shard_map/dot_general | solution.py:16
  69.8 21.4 %bitcast_add_fusion.1 = f32[512,2048]{0,1:T(8,128)S(1)} fusion(f32[1,512,2048]{1,2,0:T(8,128)S(1)} %copy-done.9, f32[2048,512]{1,0:T(8,128)S(1)} %fusion.1, s32[2048,512]{1,0:T(8,128)S(1)} %copy-done.7, f32[2,512,512]{1,2,0:T(8,128)S(1)} %copy-done.11), kind=kOutput, calls=%fused_computation.2 | convolution fusion | flops 6447693824 | bytes 17825792 | tf_op jit(solution)/shard_map/dot_general | solution.py:16
  91.2 4.3 fusion.13
  95.6 20.7 %fusion = f32[2048,512]{1,0:T(8,128)S(1)} fusion(s32[2048,512]{1,0:T(8,128)S(1)} %copy-done.7, f32[2,512,512]{1,2,0:T(8,128)S(1)} %copy-done.11), kind=kOutput, calls=%fused_computation.6 | convolution fusion | flops 6445596672 | bytes 9437184 | tf_op jit(solution)/shard_map/dot_general | solution.py:16
  116.3 21.8 %bitcast_add_fusion = f32[512,2048]{0,1:T(8,128)S(1)} fusion(f32[1,512,2048]{1,2,0:T(8,128)S(1)} %copy-done.8, f32[2048,512]{1,0:T(8,128)S(1)} %fusion, s32[2048,512]{1,0:T(8,128)S(1)} %copy-done.7, f32[2,512,512]{1,2,0:T(8,128)S(1)} %copy-done.11), kind=kOutput, calls=%fused_computation.1 | convolution fusion | flops 6447693824 | bytes 17825792 | tf_op jit(solution)/shard_map/dot_general | solution.py:16
  138.1 3.9 fusion.12
  143.2 118.4 %all-reduce.6.cloned.1.call-done = f32[512,256]{0,1:T(8,128)} async-done(((f32[512,256]{0,1:T(8,128)}), f32[512,256]{0,1:T(8,128)}) %all-reduce.6.cloned.1.call-update) | async-done | bytes 524304 | tf_op jit(solution)/shard_map/psum | solution.py:77
  263.0 6.5 fusion.27
  269.4 3.9 fusion.26
  275.2 88.9 %all-reduce.8.cloned.1.call-done = f32[2048,256]{0,1:T(8,128)} async-done(((f32[2048,256]{0,1:T(8,128)}), f32[2048,256]{0,1:T(8,128)}) %all-reduce.8.cloned.1.call-update) | async-done | bytes 2097168 | tf_op jit(solution)/shard_map/psum | solution.py:84
  366.3 6.1 fusion.15
  372.5 4.0 fusion.14
  377.4 122.4 %all-reduce.10.cloned.1.call-done = f32[512,256]{0,1:T(8,128)} async-done(((f32[512,256]{0,1:T(8,128)}), f32[512,256]{0,1:T(8,128)}) %all-reduce.10.cloned.1.call-update) | async-done | bytes 524304 | tf_op jit(solution)/shard_map/psum | solution.py:77
  501.2 6.5 fusion.25
  507.7 3.9 fusion.24
  513.5 7.7 %pad_maximum_fusion = f32[2,512,2048]{1,2,0:T(8,128)} fusion(f32[1,512,2048]{1,2,0:T(8,128)} %bitcast.39, f32[1,512,2048]{1,2,0:T(8,128)} %bitcast.38), kind=kLoop, calls=%fused_computation | loop fusion | flops 2097152 | bytes 16777216 | tf_op jit(solution)/shard_map/stack | solution.py:113
  521.3 8.9 %copy.11 = f32[2,512,2048]{2,1,0:T(8,128)} copy(f32[2,512,2048]{1,2,0:T(8,128)} %pad_maximum_fusion) | data formatting | bytes 16777216
  530.2 72.3 %all-reduce.12.cloned.1.call-done = f32[2048,256]{0,1:T(8,128)} async-done(((f32[2048,256]{0,1:T(8,128)}), f32[2048,256]{0,1:T(8,128)}) %all-reduce.12.cloned.1.call-update) | async-done | bytes 2097168 | tf_op jit(solution)/shard_map/psum | solution.py:84
  606.4 3.8 fusion.56
  617.3 120.2 %all-reduce.14.cloned.1.call-done = f32[512,256]{0,1:T(8,128)} async-done(((f32[512,256]{0,1:T(8,128)}), f32[512,256]{0,1:T(8,128)}) %all-reduce.14.cloned.1.call-update) | async-done | bytes 524304 | tf_op jit(solution)/shard_map/psum | solution.py:77
  (68 shorter events, 28.1 us)
Async XLA Ops:
  7.2 40.0 %all-gather.2.cloned.1.call-start = ((), (), s32[]{:S(2)}) async-start(), calls=%async_computation | async-start | bytes 2228224 | tf_op jit(solution)/shard_map/all_gather | solution.py:99
  7.9 253.7 %all-reduce.6.cloned.1.call-start = ((), (), s32[]{:S(2)}) async-start(), calls=%async_computation.1 | async-start | bytes 1048576 | tf_op jit(solution)/shard_map/psum | solution.py:77
  21.3 5.5 copy-start.14
  47.2 22.6 %copy-start.7 = (s32[2048,512]{1,0:T(8,128)S(1)}, s32[2048,512]{1,0:T(8,128)}, u32[]{:S(2)}) copy-start(s32[2048,512]{1,0:T(8,128)} %param.7) | copy-start | bytes 12582916
  47.2 22.6 %copy-start.9 = (f32[1,512,2048]{1,2,0:T(8,128)S(1)}, f32[1,512,2048]{1,2,0:T(8,128)}, u32[]{:S(2)}) copy-start(f32[1,512,2048]{1,2,0:T(8,128)} %copy.14) | copy-start | bytes 12582916
  47.2 22.6 %copy-start.11 = (f32[2,512,512]{1,2,0:T(8,128)S(1)}, f32[2,512,512]{1,2,0:T(8,128)}, u32[]{:S(2)}) copy-start(f32[2,512,512]{1,2,0:T(8,128)} %all-gather.2.cloned.1.call-done) | copy-start | bytes 6291460
  91.2 4.4 copy-start
  95.6 20.7 %copy-start.8 = (f32[1,512,2048]{1,2,0:T(8,128)S(1)}, f32[1,512,2048]{1,2,0:T(8,128)}, u32[]{:S(2)}) copy-start(f32[1,512,2048]{1,2,0:T(8,128)} %copy.15) | copy-start | bytes 12582916
  138.1 3.9 copy-start.2
  138.1 4.9 copy-start.15
  143.0 221.1 %all-reduce.8.cloned.1.call-start = ((), (), s32[]{:S(2)}) async-start(), calls=%async_computation.2 | async-start | bytes 4194304 | tf_op jit(solution)/shard_map/psum | solution.py:84
  261.6 7.8 %copy-start.3 = (f32[512,2048]{0,1:T(8,128)S(1)}, f32[512,2048]{0,1:T(8,128)}, u32[]{:S(2)}) copy-start(f32[512,2048]{0,1:T(8,128)} %copy-done.2) | copy-start | bytes 12582916
  261.6 7.8 %copy-start.12 = (f32[512,256]{0,1:T(8,128)S(1)}, f32[512,256]{0,1:T(8,128)}, u32[]{:S(2)}) copy-start(f32[512,256]{0,1:T(8,128)} %all-reduce.6.cloned.1.call-done) | copy-start | bytes 1572868
  275.2 224.7 %all-reduce.10.cloned.1.call-start = ((), (), s32[]{:S(2)}) async-start(), calls=%async_computation.3 | async-start | bytes 1048576 | tf_op jit(solution)/shard_map/psum | solution.py:77
  364.1 2.2 copy-start.10
  366.3 6.2 copy-start.4
  377.4 225.1 %all-reduce.12.cloned.1.call-start = ((), (), s32[]{:S(2)}) async-start(), calls=%async_computation.4 | async-start | bytes 4194304 | tf_op jit(solution)/shard_map/psum | solution.py:84
  499.8 7.9 %copy-start.5 = (f32[512,2048]{0,1:T(8,128)S(1)}, f32[512,2048]{0,1:T(8,128)}, u32[]{:S(2)}) copy-start(f32[512,2048]{0,1:T(8,128)} %copy-done.2) | copy-start | bytes 12582916
  499.8 7.9 %copy-start.13 = (f32[512,256]{0,1:T(8,128)S(1)}, f32[512,256]{0,1:T(8,128)}, u32[]{:S(2)}) copy-start(f32[512,256]{0,1:T(8,128)} %all-reduce.10.cloned.1.call-done) | copy-start | bytes 1572868
  513.5 224.1 %all-reduce.14.cloned.1.call-start = ((), (), s32[]{:S(2)}) async-start(), calls=%async_computation.5 | async-start | bytes 1048576 | tf_op jit(solution)/shard_map/psum | solution.py:77
  602.5 3.9 copy-start.1
  606.4 3.9 copy-start.6
Sparse Core Ops, SparseCore 0:
  9.6 37.4 all-gather.1
  143.1 118.4 all-reduce.5
  275.3 88.7 all-reduce.7
  377.5 122.3 all-reduce.9
  513.6 88.8 all-reduce.11
  615.2 122.3 all-reduce.13
where the time goes:
time: 756 us; the launch traced here: 747 us
  waiting for transfers between devices  540 us (71%)
  matrix products  133 us (18%)
  local copies, waits for them, and re-layouts  35.9 us (5%)
  other arithmetic  23 us (3%)
  between operations  15 us (2%)
    psum x3, waiting for transfers between devices, camera_pass(): camera = lax.psum(camera_rows(real_new, imag_new, slm_now, width), 'mode')  361 us
    psum x2, waiting for transfers between devices, slm_pass(): back_field = lax.psum(slm_rows(real_new, imag_new, shaped, width), 'pix')  161 us
    dot_general x4, matrix products, matmul_nt(): lax.dot_general(left, right, (((1,), (1,)), ((), ())), precision=lax.Prec...  86.5 us
    dot_general x6, matrix products, matmul(): jnp.dot(left, right, precision=lax.Precision.HIGHEST, preferred_element_t...  26 us
    unnamed x38, local copies, waits for them, and re-layouts  23 us
    dot_general x4, matrix products, matmul_tn(): lax.dot_general(left, right, (((0,), (0,)), ((), ())), precision=lax.Prec...  20.8 us
    all_gather x1, waiting for transfers between devices, body(): panel_whole = lax.all_gather(calibration_fields, 'mode', axis=2, tiled=True)  16.7 us
  transfers between devices with their start and end apart: 6, of which 6 were waited for; matrix products, arithmetic and copies ran while one was open for 6% of the time, Pallas kernels for 0%

commit v1 on v0

--- a/solution.py
+++ b/solution.py
@@ -81,7 +81,7 @@
 
 
 def slm_pass(real_new, imag_new, shaped, floor_value, width):
-    back_field = lax.psum(slm_rows(real_new, imag_new, shaped, width), "pix")
+    back_field = jnp.sum(lax.all_gather(slm_rows(real_new, imag_new, shaped, width), "pix"), axis=0)
     slm_now = normalize(back_field, floor_value, width)
     return slm_now
 

time: 756 us -> 980 us (1.30)
  waiting for transfers between devices: 540 us -> 723 us
  local copies, waits for them, and re-layouts: 35.9 us -> 72.8 us
    all_gather x0 -> x2, waiting for transfers between devices: none -> 354 us  [slm_pass(): lax.all_gather(slm_rows(real_new, imag_new, shaped, width), 'pix')]
    psum x2 -> x0, waiting for transfers between devices: 161 us -> none  [slm_pass(): back_field = lax.psum(slm_rows(real_new, imag_new, shaped, width), 'pix')]
    unnamed x38 -> x40, local copies, waits for them, and re-layouts: 23 us -> 60 us
    reduce_sum x0 -> x2, other arithmetic: none -> 11.2 us  [slm_pass(): jnp.sum(lax.all_gather(slm_rows(real_new, imag_new, shaped, width), 'pix'...]
  transfers between devices with their start and end apart: 6 -> 6, of which waited for: 6 -> 6; matrix products, arithmetic and copies ran while one was open for 6% -> 4% of each run, Pallas kernels for 0% -> 0%
where the time goes in v1:
time: 980 us; the launch traced here: 971 us
  waiting for transfers between devices  723 us (74%)
  matrix products  131 us (13%)
  local copies, waits for them, and re-layouts  72.8 us (7%)
  other arithmetic  29.2 us (3%)
  between operations  15 us (2%)
    all_gather x2, waiting for transfers between devices, slm_pass(): lax.all_gather(slm_rows(real_new, imag_new, shaped, width), 'pix')  354 us
    psum x3, waiting for transfers between devices, camera_pass(): camera = lax.psum(camera_rows(real_new, imag_new, slm_now, width), 'mode')  351 us
    dot_general x4, matrix products, matmul_nt(): lax.dot_general(left, right, (((1,), (1,)), ((), ())), precision=lax.Prec...  86.6 us
    unnamed x40, local copies, waits for them, and re-layouts  60 us
    dot_general x6, matrix products, matmul(): jnp.dot(left, right, precision=lax.Precision.HIGHEST, preferred_element_t...  23.7 us
    dot_general x4, matrix products, matmul_tn(): lax.dot_general(left, right, (((0,), (0,)), ((), ())), precision=lax.Prec...  20.9 us
  transfers between devices with their start and end apart: 6, of which 6 were waited for; matrix products, arithmetic and copies ran while one was open for 4% of the time, Pallas kernels for 0%

profile of v1, /device:TPU:1, one launch (start us, length us, event | category | flops | bytes accessed | tf_op | source)
XLA Modules:
  0.0 971.3 jit_solution(8058897451236706472)
XLA Ops:
  7.9 7.9 fusion.54
  15.8 5.5 copy.19
  21.3 5.5 copy.20
  30.5 16.7 %all-gather.6.cloned.1.call-done = f32[2,512,512]{1,2,0:T(8,128)} async-done(((f32[2,512,32]{1,2,0:T(8,128)}), f32[2,512,512]{1,2,0:T(8,128)}) %all-gather.6.cloned.1.call-update) | async-done | bytes 2097168 | tf_op jit(solution)/shard_map/all_gather | solution.py:99
  47.2 22.8 %fusion.1 = f32[2048,512]{1,0:T(8,128)S(1)} fusion(s32[2048,512]{1,0:T(8,128)} %param.7, f32[2,512,512]{1,2,0:T(8,128)} %all-gather.6.cloned.1.call-done), kind=kOutput, calls=%fused_computation.9 | convolution fusion | flops 6445596672 | bytes 9437184 | tf_op jit(solution)/shard_map/dot_general | solution.py:16
  70.0 21.4 %bitcast_add_fusion.1 = f32[512,2048]{0,1:T(8,128)S(1)} fusion(f32[1,512,2048]{1,2,0:T(8,128)S(1)} %copy-done.10, f32[2048,512]{1,0:T(8,128)S(1)} %fusion.1, s32[2048,512]{1,0:T(8,128)S(1)} %copy-done.8, f32[2,512,512]{1,2,0:T(8,128)S(1)} %copy-done.11), kind=kOutput, calls=%fused_computation.4 | convolution fusion | flops 6447693824 | bytes 17825792 | tf_op jit(solution)/shard_map/dot_general | solution.py:16
  91.4 4.2 fusion.13
  95.5 21.0 %fusion = f32[2048,512]{1,0:T(8,128)S(1)} fusion(s32[2048,512]{1,0:T(8,128)S(1)} %copy-done.8, f32[2,512,512]{1,2,0:T(8,128)S(1)} %copy-done.11), kind=kOutput, calls=%fused_computation.8 | convolution fusion | flops 6445596672 | bytes 9437184 | tf_op jit(solution)/shard_map/dot_general | solution.py:16
  116.5 21.6 %bitcast_add_fusion = f32[512,2048]{0,1:T(8,128)S(1)} fusion(f32[1,512,2048]{1,2,0:T(8,128)S(1)} %copy-done.9, f32[2048,512]{1,0:T(8,128)S(1)} %fusion, s32[2048,512]{1,0:T(8,128)S(1)} %copy-done.8, f32[2,512,512]{1,2,0:T(8,128)S(1)} %copy-done.11), kind=kOutput, calls=%fused_computation.3 | convolution fusion | flops 6447693824 | bytes 17825792 | tf_op jit(solution)/shard_map/dot_general | solution.py:16
  143.2 118.4 %all-reduce.4.cloned.1.call-done = f32[512,256]{0,1:T(8,128)} async-done(((f32[512,256]{0,1:T(8,128)}), f32[512,256]{0,1:T(8,128)}) %all-reduce.4.cloned.1.call-update) | async-done | bytes 524304 | tf_op jit(solution)/shard_map/psum | solution.py:77
  262.9 6.6 fusion.26
  275.4 185.5 %all-gather.8.cloned.1.call-done = f32[16384,256]{0,1:T(8,128)} async-done(((f32[2048,256]{0,1:T(8,128)}), f32[16384,256]{0,1:T(8,128)}) %all-gather.8.cloned.1.call-update) | async-done | bytes 16777232 | tf_op jit(solution)/shard_map/all_gather | solution.py:84
  460.9 17.6 %copy.21 = f32[32,8,8,2048]{3,2,1,0:T(8,128)S(1)} copy(f32[32,8,8,2048]{3,1,2,0:T(8,128)} %bitcast.51) | data formatting | bytes 33554432
  478.5 5.6 bitcast_reduce_fusion.1
  484.5 4.0 fusion.14
  488.4 4.0 fusion.15
  493.4 117.6 %all-reduce.6.cloned.1.call-done = f32[512,256]{0,1:T(8,128)} async-done(((f32[512,256]{0,1:T(8,128)}), f32[512,256]{0,1:T(8,128)}) %all-reduce.6.cloned.1.call-update) | async-done | bytes 524304 | tf_op jit(solution)/shard_map/psum | solution.py:77
  612.3 6.4 fusion.24
  624.6 7.7 pad_maximum_fusion
  632.3 9.4 copy.16
  641.7 168.4 %all-gather.10.cloned.1.call-done = f32[16384,256]{0,1:T(8,128)} async-done(((f32[2048,256]{0,1:T(8,128)}), f32[16384,256]{0,1:T(8,128)}) %all-gather.10.cloned.1.call-update) | async-done | bytes 16777232 | tf_op jit(solution)/shard_map/all_gather | solution.py:84
  810.1 17.6 %copy.22 = f32[32,8,8,2048]{3,2,1,0:T(8,128)S(1)} copy(f32[32,8,8,2048]{3,1,2,0:T(8,128)} %bitcast.50) | data formatting | bytes 33554432
  827.7 5.7 bitcast_reduce_fusion
  846.5 115.4 %all-reduce.8.cloned.1.call-done = f32[512,256]{0,1:T(8,128)} async-done(((f32[512,256]{0,1:T(8,128)}), f32[512,256]{0,1:T(8,128)}) %all-reduce.8.cloned.1.call-update) | async-done | bytes 524304 | tf_op jit(solution)/shard_map/psum | solution.py:77
  (72 shorter events, 40.2 us)
Async XLA Ops:
  7.2 40.0 %all-gather.6.cloned.1.call-start = ((), (), s32[]{:S(2)}) async-start(), calls=%async_computation | async-start | bytes 2228224 | tf_op jit(solution)/shard_map/all_gather | solution.py:99
  7.9 253.7 %all-reduce.4.cloned.1.call-start = ((), (), s32[]{:S(2)}) async-start(), calls=%async_computation.1 | async-start | bytes 1048576 | tf_op jit(solution)/shard_map/psum | solution.py:77
  21.3 5.5 copy-start.14
  47.2 22.8 %copy-start.8 = (s32[2048,512]{1,0:T(8,128)S(1)}, s32[2048,512]{1,0:T(8,128)}, u32[]{:S(2)}) copy-start(s32[2048,512]{1,0:T(8,128)} %param.7) | copy-start | bytes 12582916
  47.2 22.8 %copy-start.10 = (f32[1,512,2048]{1,2,0:T(8,128)S(1)}, f32[1,512,2048]{1,2,0:T(8,128)}, u32[]{:S(2)}) copy-start(f32[1,512,2048]{1,2,0:T(8,128)} %copy.19) | copy-start | bytes 12582916
  47.2 22.8 %copy-start.11 = (f32[2,512,512]{1,2,0:T(8,128)S(1)}, f32[2,512,512]{1,2,0:T(8,128)}, u32[]{:S(2)}) copy-start(f32[2,512,512]{1,2,0:T(8,128)} %all-gather.6.cloned.1.call-done) | copy-start | bytes 6291460
  91.3 4.2 copy-start
  95.5 21.0 %copy-start.9 = (f32[1,512,2048]{1,2,0:T(8,128)S(1)}, f32[1,512,2048]{1,2,0:T(8,128)}, u32[]{:S(2)}) copy-start(f32[1,512,2048]{1,2,0:T(8,128)} %copy.20) | copy-start | bytes 12582916
  138.1 3.9 copy-start.5
  138.1 4.9 copy-start.15
  143.0 317.9 %all-gather.8.cloned.1.call-start = ((), (), s32[]{:S(2)}) async-start(), calls=%async_computation.4 | async-start | bytes 18874368 | tf_op jit(solution)/shard_map/all_gather | solution.py:84
  261.6 8.0 copy-start.1
  261.6 8.0 copy-start.12
  275.3 335.7 %all-reduce.6.cloned.1.call-start = ((), (), s32[]{:S(2)}) async-start(), calls=%async_computation.2 | async-start | bytes 1048576 | tf_op jit(solution)/shard_map/psum | solution.py:77
  478.5 6.0 copy-start.6
  484.5 4.0 copy-start.2
  493.3 316.8 %all-gather.10.cloned.1.call-start = ((), (), s32[]{:S(2)}) async-start(), calls=%async_computation.5 | async-start | bytes 18874368 | tf_op jit(solution)/shard_map/all_gather | solution.py:84
  611.0 7.8 copy-start.3
  611.0 7.8 copy-start.13
  624.5 337.3 %all-reduce.8.cloned.1.call-start = ((), (), s32[]{:S(2)}) async-start(), calls=%async_computation.3 | async-start | bytes 1048576 | tf_op jit(solution)/shard_map/psum | solution.py:77
  833.4 2.2 copy-start.4
  835.6 3.9 copy-start.7
Sparse Core Ops, SparseCore 0:
  9.6 37.4 all-gather.5
  143.1 118.4 all-reduce.3
  275.4 185.3 all-gather.7
  493.5 117.4 all-reduce.5
  624.6 185.4 all-gather.9
  844.3 117.4 all-reduce.7
